TPU v7x, 512 devices: a whole 4x4x16 slice. The times are simulated.
512 devices in a mesh: ctx: 64 (over z, x), ch: 8 (over y, core).
Axes of the slice: x: 4, y: 4, z: 16, core: 2. Of those that a mesh axis runs over, the one named last changes fastest.
Arguments:
- gate_input: bfloat16 [16384, 4096], P('ctx', 'ch'), may hold values from -6 to 6
- key_input: bfloat16 [16384, 4096], P('ctx', 'ch'), may hold values from -6 to 6
- value_input: bfloat16 [16384, 4096], P('ctx', 'ch'), may hold values from -6 to 6
- decay_rate: float32 [16, 4096], P(None, 'ch'), may hold values from 0.00012207031 to 0.26666667
- frequency: float32 [16, 4096], P(None, 'ch'), may hold values from 0 to 2.4
- residue: float32 [2, 16, 4096], P(None, None, 'ch'), may hold values from -2 to 2
- skip_gain: float32 [4096], P('ch'), may hold values from -3 to 3
- out_weight: bfloat16 [4096, 4096], P('ctx', 'ch'), may hold values from -0.09375 to 0.09375
Outputs:
- mixed: bfloat16 [16384, 4096], P('ctx', 'ch')
All inputs are finite; a program needn't handle non-finite values.
Results may differ from a plain program's by a relative error of at most 0.014.
Values may be sent and summed in bfloat16 or wider, within the bound.
A program may use at most 128 MiB of HBM per device.

v0:
```python
import jax
import jax.numpy as jnp
from jax import lax
from jax.sharding import PartitionSpec as P


def entering(value, axis, join, neutral):
    count, mine = (lax.axis_size(axis), lax.axis_index(axis))
    pieces = jax.tree.map(lambda part: lax.all_gather(part, axis), value)
    so_far = jax.tree.map(
        lambda part, zero: jnp.full_like(part, 0) + jnp.asarray(zero, part.dtype), value, neutral
    )

    def hop(position, so_far):
        longer = join(so_far, jax.tree.map(lambda part: part[position], pieces))
        return jax.tree.map(lambda new, old: jnp.where(position < mine, new, old), longer, so_far)

    return lax.fori_loop(0, count - 1, hop, so_far)


def cmul(a_re, a_im, b_re, b_im):
    return (a_re * b_re - a_im * b_im, a_re * b_im + a_im * b_re)


def filter_tables(decay_rate, frequency, residue, block_len):
    damping = 0.125 * decay_rate
    turning = 0.125 * frequency
    scaling = jnp.sqrt(2.0 * damping)
    coef_re = scaling * residue[0]
    coef_im = scaling * residue[1]
    offsets = jnp.arange(block_len).astype(jnp.float32)

    def powers(counts):
        fading = jnp.exp(-damping[None] * counts[:, None, None])
        phase = turning[None] * counts[:, None, None]
        return (fading * jnp.cos(phase), fading * jnp.sin(phase))

    back_re, back_im = powers(block_len - 1.0 - offsets)
    ahead_re, ahead_im = powers(offsets + 1.0)
    out_re, out_im = cmul(coef_re[None], coef_im[None], ahead_re, ahead_im)
    lag_re, lag_im = powers(offsets)
    filt = jnp.sum(coef_re[None] * lag_re - coef_im[None] * lag_im, axis=1)
    places = jnp.arange(block_len)
    differ = places[:, None] - places[None, :]
    picked = jnp.take(filt, jnp.maximum(differ, 0), axis=0)
    toeplitz = jnp.where((differ >= 0)[:, :, None], picked, jnp.zeros_like(picked))
    jump_re, jump_im = powers(jnp.full((1,), block_len).astype(jnp.float32))
    return (back_re, back_im, out_re, out_im, toeplitz, jump_re[0], jump_im[0])


def chain(earlier, later):
    sum_re, sum_im = cmul(earlier[0], earlier[1], later[2], later[3])
    pow_re, pow_im = cmul(earlier[2], earlier[3], later[2], later[3])
    return (sum_re + later[0], sum_im + later[1], pow_re, pow_im)


def on_device(
    gate_input, key_input, value_input, decay_rate, frequency, residue, skip_gain, out_weight
):
    highest = lax.Precision.HIGHEST
    signal = key_input.astype(jnp.float32) * value_input.astype(jnp.float32)
    tok_len, chans = signal.shape
    block_len = 16
    block_count = tok_len // block_len
    back_re, back_im, out_re, out_im, toeplitz, jump_re, jump_im = filter_tables(
        decay_rate, frequency, residue, block_len
    )
    blocks = signal.reshape(block_count, block_len, chans)
    entry_re = jnp.einsum("snc,bsc->bnc", back_re, blocks, precision=highest)
    entry_im = jnp.einsum("snc,bsc->bnc", back_im, blocks, precision=highest)

    def advance(state, entry):
        moved_re, moved_im = cmul(jump_re, jump_im, state[0], state[1])
        grown_re, grown_im = cmul(state[2], state[3], jump_re, jump_im)
        return ((moved_re + entry[0], moved_im + entry[1], grown_re, grown_im), state)

    zeros = jnp.zeros(jump_re.shape, jnp.float32)
    ones = jnp.ones(jump_re.shape, jnp.float32)
    final, starts = lax.scan(advance, (zeros, zeros, ones, zeros), (entry_re, entry_im))
    local_re, local_im, device_re, device_im = final
    prefix = entering(
        (local_re, local_im, device_re, device_im), "ctx", chain, (zeros, zeros, ones, zeros)
    )
    incoming_re, incoming_im = (prefix[0], prefix[1])
    carried_re, carried_im = cmul(starts[2], starts[3], incoming_re[None], incoming_im[None])
    begin_re = starts[0] + carried_re
    begin_im = starts[1] + carried_im
    far = jnp.einsum("tnc,bnc->btc", out_re, begin_re, precision=highest) - jnp.einsum(
        "tnc,bnc->btc", out_im, begin_im, precision=highest
    )
    near = jnp.einsum("tsc,bsc->btc", toeplitz, blocks, precision=highest)
    conv = (near + far).reshape(tok_len, chans)
    gated = (gate_input.astype(jnp.float32) * (conv + skip_gain[None, :] * signal)).astype(
        jnp.bfloat16
    )
    whole = lax.all_gather(gated, "ch", axis=1, tiled=True)
    all_rows = lax.all_gather(out_weight, "ctx", axis=0, tiled=True)
    mixed = jnp.dot(whole, all_rows, preferred_element_type=jnp.float32)
    return mixed.astype(jnp.bfloat16)


def solution(mesh):
    placed = (
        P("ctx", "ch"),
        P("ctx", "ch"),
        P("ctx", "ch"),
        P(None, "ch"),
        P(None, "ch"),
        P(None, None, "ch"),
        P("ch"),
        P("ctx", "ch"),
    )
    return jax.shard_map(
        on_device, mesh=mesh, in_specs=placed, out_specs=P("ctx", "ch"), check_vma=False
    )
```

profile of v0, /device:TPU:8, one launch (start us, length us, event | category | flops | bytes accessed | tf_op | source)
XLA Modules:
  0.0 906.5 jit_solution(10265172625318404622)
XLA Ops:
  6.6 1.1 convert_multiply_fusion
  7.7 3.7 copy.51
  11.5 6.1 multiply_add_fusion.1
  17.6 4.1 copy.54
  21.8 9.9 %convolution_bitcast_fusion.1 = f32[16,16,512]{1,0,2:T(8,128)} fusion(f32[16,16,512]{1,0,2:T(8,128)} %copy.51, f32[16,16,512]{1,0,2:T(8,128)} %copy.54), kind=kOutput, calls=%fused_computation.21 | convolution fusion | flops 25165824 | bytes 1572864 | tf_op jit(solution)/shard_map/snc,bsc->bnc/dot_general | solution.py:69
  31.7 3.5 copy.57
  35.2 3.7 copy.56
  38.9 9.9 %convolution_bitcast_fusion = f32[16,16,512]{1,0,2:T(8,128)} fusion(f32[16,16,512]{1,0,2:T(8,128)} %copy.51, f32[16,16,512]{1,0,2:T(8,128)} %copy.56), kind=kOutput, calls=%fused_computation.20 | convolution fusion | flops 25165824 | bytes 1572864 | tf_op jit(solution)/shard_map/snc,bsc->bnc/dot_general | solution.py:70
  48.8 3.5 copy.58
  52.5 14.0 %while.41 = (s32[]{:T(128)}, f32[16,512]{1,0:T(8,128)S(1)}, f32[16,512]{1,0:T(8,128)S(1)}, f32[16,512]{1,0:T(8,128)S(1)}, f32[16,512]{1,0:T(8,128)S(1)}, /*index...) while((s32[]{:T(128)}, f32[16,512]{1,0:T(8,128)S(1)}, ...), condition=%wide.region_2.3_spmd.clone, body=%wide.region_1.2_spmd.clone.sunk | while | flops 180227 | bytes 655533 | solution.py:79
  69.6 1.8 gather_fusion
  71.4 2.0 select_select_fusion
  73.4 4.5 copy.52
  77.9 3.6 copy.60
  81.5 3.7 copy.62
  85.2 12.3 %fusion.17 = f32[512,16,16]{2,1,0:T(8,128)} fusion(f32[16,16,512]{1,0,2:T(8,128)} %copy.51, f32[16,16,512]{1,0,2:T(8,128)} %copy.52), kind=kOutput, calls=%fused_computation.66 | convolution fusion | flops 25165824 | bytes 1572864 | tf_op jit(solution)/shard_map/tsc,bsc->btc/dot_general | solution.py:91
  97.5 115.2 %all-gather.15.cloned.1.call-done = f32[1024,512]{1,0:T(8,128)} async-done(((f32[16,512]{1,0:T(8,128)}), f32[1024,512]{1,0:T(8,128)}) %all-gather.15.cloned.1.call-update) | async-done | bytes 2097168 | tf_op jit(solution)/shard_map/all_gather | solution.py:9
  212.7 139.9 %all-gather.17.cloned.1.call-done = f32[1024,512]{1,0:T(8,128)} async-done(((f32[16,512]{1,0:T(8,128)}), f32[1024,512]{1,0:T(8,128)}) %all-gather.17.cloned.1.call-update) | async-done | bytes 2097168 | tf_op jit(solution)/shard_map/all_gather | solution.py:9
  352.6 139.9 %all-gather.19.cloned.1.call-done = f32[1024,512]{1,0:T(8,128)} async-done(((f32[16,512]{1,0:T(8,128)}), f32[1024,512]{1,0:T(8,128)}) %all-gather.19.cloned.1.call-update) | async-done | bytes 2097168 | tf_op jit(solution)/shard_map/all_gather | solution.py:9
  492.5 139.8 %all-gather.21.cloned.1.call-done = f32[1024,512]{1,0:T(8,128)} async-done(((f32[16,512]{1,0:T(8,128)}), f32[1024,512]{1,0:T(8,128)}) %all-gather.21.cloned.1.call-update) | async-done | bytes 2097168 | tf_op jit(solution)/shard_map/all_gather | solution.py:9
  632.3 54.2 %while.42 = (s32[]{:T(128)}, f32[16,512]{1,0:T(8,128)S(1)}, f32[16,512]{1,0:T(8,128)S(1)}, s32[]{:T(128)}, f32[64,16,512]{2,1,0:T(8,128)}, /*index=5*/f32[64,16,...) while((s32[]{:T(128)}, f32[16,512]{1,0:T(8,128)S(1)}, ...), condition=%wide.region_4.5_spmd.clone, body=%wide.region_3.4_spmd.clone.sunk | while | flops 98308 | bytes 262277 | solution.py:18
  643.5 0.9 fusion.32
  644.3 0.8 fusion.32
  645.2 0.8 fusion.32
  646.1 0.8 fusion.32
  646.9 0.8 fusion.32
  647.8 0.8 fusion.32
  648.6 0.8 fusion.32
  649.5 0.8 fusion.32
  650.4 0.8 fusion.32
  651.2 0.8 fusion.32
  652.1 0.8 fusion.32
  652.9 0.8 fusion.32
  653.8 0.8 fusion.32
  654.7 0.8 fusion.32
  655.5 0.8 fusion.32
  656.4 0.8 fusion.32
  657.2 0.8 fusion.32
  658.1 0.8 fusion.32
  686.8 3.7 copy.59
  690.4 3.6 copy.61
  694.1 9.5 %fusion.18 = f32[512,16,16]{2,1,0:T(8,128)S(1)} fusion(f32[16,16,512]{1,0,2:T(8,128)} %copy.59, f32[16,16,512]{1,0,2:T(8,128)} %copy.60), kind=kOutput, calls=%fused_computation.67 | convolution fusion | flops 25165824 | bytes 1572864 | tf_op jit(solution)/shard_map/tnc,bnc->btc/dot_general | solution.py:88
  703.6 8.5 add_bitcast_fusion
  712.1 2.9 copy.63
  715.0 0.8 fusion.15
  716.5 27.5 %all-gather.11.cloned.1.call-done = bf16[256,4096]{1,0:T(8,128)(2,1)} async-done(((bf16[256,512]{1,0:T(8,128)(2,1)}), bf16[256,4096]{1,0:T(8,128)(2,1)}) %all-gather.11.cloned.1.call-update) | async-done | bytes 2097168 | tf_op jit(solution)/shard_map/all_gather | solution.py:96
  744.0 150.7 %all-gather.13.cloned.1.call-done = bf16[4096,512]{1,0:T(8,128)(2,1)} async-done(((bf16[64,512]{1,0:T(8,128)(2,1)}), bf16[4096,512]{1,0:T(8,128)(2,1)}) %all-gather.13.cloned.1.call-update) | async-done | bytes 4194320 | tf_op jit(solution)/shard_map/all_gather | solution.py:97
  894.6 4.8 convolution_convert_fusion
  (151 shorter events, 55.3 us)
Async XLA Ops:
  6.5 4.8 copy-start.11
  6.5 4.8 copy-start.12
  6.5 4.8 copy-start.10
  6.5 206.1 %all-gather.15.cloned.1.call-start = ((), (), s32[]{:S(2)}) async-start(), calls=%async_computation.2 | async-start | bytes 2129920 | tf_op jit(solution)/shard_map/all_gather | solution.py:9
  66.5 0.6 copy-start.5
  66.6 0.7 copy-start.6
  66.6 1.4 copy-start.3
  66.6 2.1 copy-start.4
  67.2 285.4 %all-gather.17.cloned.1.call-start = ((), (), s32[]{:S(2)}) async-start(), calls=%async_computation.3 | async-start | bytes 2129920 | tf_op jit(solution)/shard_map/all_gather | solution.py:9
  67.9 424.6 %all-gather.19.cloned.1.call-start = ((), (), s32[]{:S(2)}) async-start(), calls=%async_computation.4 | async-start | bytes 2129920 | tf_op jit(solution)/shard_map/all_gather | solution.py:9
  68.7 563.6 %all-gather.21.cloned.1.call-start = ((), (), s32[]{:S(2)}) async-start(), calls=%async_computation.5 | async-start | bytes 2129920 | tf_op jit(solution)/shard_map/all_gather | solution.py:9
  69.2 674.7 %all-gather.11.cloned.1.call-start = ((), (), s32[]{:S(2)}) async-start(), calls=%async_computation | async-start | bytes 2359296 | tf_op jit(solution)/shard_map/all_gather | solution.py:96
  694.1 9.5 %copy-start = (f32[512,16,16]{2,1,0:T(8,128)S(1)}, f32[512,16,16]{2,1,0:T(8,128)}, u32[]{:S(2)}) copy-start(f32[512,16,16]{2,1,0:T(8,128)} %fusion.17) | copy-start | bytes 1572868
  694.1 9.5 %copy-start.1 = (f32[16,16,512]{1,0,2:T(8,128)S(1)}, f32[16,16,512]{1,0,2:T(8,128)}, u32[]{:S(2)}) copy-start(f32[16,16,512]{1,0,2:T(8,128)} %copy.62) | copy-start | bytes 1572868
  694.1 9.5 %copy-start.2 = (f32[16,16,512]{1,0,2:T(8,128)S(1)}, f32[16,16,512]{1,0,2:T(8,128)}, u32[]{:S(2)}) copy-start(f32[16,16,512]{1,0,2:T(8,128)} %copy.61) | copy-start | bytes 1572868
  712.1 2.9 copy-start.7
  712.1 2.9 copy-start.8
  712.1 2.9 copy-start.9
  712.1 2.9 copy-start.13
  715.9 178.7 %all-gather.13.cloned.1.call-start = ((), (), s32[]{:S(2)}) async-start(), calls=%async_computation.1 | async-start | bytes 4259840 | tf_op jit(solution)/shard_map/all_gather | solution.py:97
Sparse Core Ops, SparseCore 0:
  67.3 145.3 all-gather.14
  215.6 136.9 all-gather.16
  355.5 136.9 all-gather.18
  495.3 136.9 all-gather.20
  716.0 27.8 all-gather.10
  746.8 147.8 all-gather.12
where the time goes:
time: 918 us; the launch traced here: 906 us
  waiting for transfers between devices  715 us (78%)
  other arithmetic  76.7 us (8%)
  matrix products  54.8 us (6%)
  local copies, waits for them, and re-layouts  43.3 us (5%)
  between operations  14 us (2%)
    all_gather x4, waiting for transfers between devices, entering(): pieces = jax.tree.map(lambda part: lax.all_gather(part, axis), value)  535 us
    all_gather x1, waiting for transfers between devices, on_device(): all_rows = lax.all_gather(out_weight, 'ctx', axis=0, tiled=True)  151 us
    select_n x63, other arithmetic, hop(): jnp.where(position < mine, new, old)  52.8 us
    all_gather x1, waiting for transfers between devices, on_device(): whole = lax.all_gather(gated, 'ch', axis=1, tiled=True)  27.5 us
    add x17, other arithmetic, cmul(): return (a_re * b_re - a_im * b_im, a_re * b_im + a_im * b_re)  19.1 us
  transfers between devices with their start and end apart: 6, of which 6 were waited for; matrix products, arithmetic and copies ran while one was open for 3% of the time, Pallas kernels for 0%

commit v1 on v0

--- a/solution.py
+++ b/solution.py
@@ -94,7 +94,9 @@
         jnp.bfloat16
     )
     whole = lax.all_gather(gated, "ch", axis=1, tiled=True)
-    all_rows = lax.all_gather(out_weight, "ctx", axis=0, tiled=True)
+    all_rows = jnp.concatenate(
+        lax.all_to_all(jnp.stack([out_weight] * lax.axis_size("ctx")), "ctx", 0, 0), axis=0
+    )
     mixed = jnp.dot(whole, all_rows, preferred_element_type=jnp.float32)
     return mixed.astype(jnp.bfloat16)
 

time: 918 us -> 824 us (0.90)
  the two profiles are of different devices: /device:TPU:8 before, /device:TPU:1 now
where the time goes in v1:
time: 824 us; the launch traced here: 812 us
  waiting for transfers between devices  599 us (73%)
  other arithmetic  76.9 us (9%)
  matrix products  54.7 us (7%)
  local copies, waits for them, and re-layouts  46 us (6%)
  starting transfers between devices  19.7 us (2%)
  between operations  13.7 us (2%)
    all_gather x4, waiting for transfers between devices, entering(): pieces = jax.tree.map(lambda part: lax.all_gather(part, axis), value)  559 us
    select_n x63, other arithmetic, hop(): jnp.where(position < mine, new, old)  52.9 us
    all_gather x1, waiting for transfers between devices, on_device(): whole = lax.all_gather(gated, 'ch', axis=1, tiled=True)  38.3 us
    all_to_all x1, starting transfers between devices, on_device(): lax.all_to_all(jnp.stack([out_weight] * lax.axis_size('ctx')), 'ctx', 0, 0)  19.5 us
    add x17, other arithmetic, cmul(): return (a_re * b_re - a_im * b_im, a_re * b_im + a_im * b_re)  19.1 us
  transfers between devices with their start and end apart: 6, of which 5 were waited for; matrix products, arithmetic and copies ran while one was open for 14% of the time, Pallas kernels for 0%

profile of v1, /device:TPU:1, one launch (start us, length us, event | category | flops | bytes accessed | tf_op | source)
XLA Modules:
  0.0 812.4 jit_solution(11786041323372526939)
XLA Ops:
  6.6 1.1 convert_multiply_fusion
  7.7 3.7 copy.51
  11.6 6.1 multiply_add_fusion.1
  17.7 4.2 copy.54
  21.8 9.9 %convolution_bitcast_fusion.1 = f32[16,16,512]{1,0,2:T(8,128)} fusion(f32[16,16,512]{1,0,2:T(8,128)} %copy.51, f32[16,16,512]{1,0,2:T(8,128)} %copy.54), kind=kOutput, calls=%fused_computation.21 | convolution fusion | flops 25165824 | bytes 1572864 | tf_op jit(solution)/shard_map/snc,bsc->bnc/dot_general | solution.py:69
  31.7 3.5 copy.57
  35.2 3.7 copy.56
  38.9 9.9 %convolution_bitcast_fusion = f32[16,16,512]{1,0,2:T(8,128)} fusion(f32[16,16,512]{1,0,2:T(8,128)} %copy.51, f32[16,16,512]{1,0,2:T(8,128)} %copy.56), kind=kOutput, calls=%fused_computation.20 | convolution fusion | flops 25165824 | bytes 1572864 | tf_op jit(solution)/shard_map/snc,bsc->bnc/dot_general | solution.py:70
  48.8 3.5 copy.58
  52.5 14.0 %while.41 = (s32[]{:T(128)}, f32[16,512]{1,0:T(8,128)S(1)}, f32[16,512]{1,0:T(8,128)S(1)}, f32[16,512]{1,0:T(8,128)S(1)}, f32[16,512]{1,0:T(8,128)S(1)}, /*index...) while((s32[]{:T(128)}, f32[16,512]{1,0:T(8,128)S(1)}, ...), condition=%wide.region_2.3_spmd.clone, body=%wide.region_1.2_spmd.clone.sunk | while | flops 180227 | bytes 655533 | solution.py:79
  69.3 2.5 stack.2
  71.8 19.5 %all-to-all-start = ((bf16[64,64,512]{2,1,0:T(8,128)(2,1)}), bf16[64,64,512]{2,1,0:T(8,128)(2,1)}, u32[]{:S(2)}, u32[]{:S(2)}) async-start(bf16[64,64,512]{2,1,0:T(8,128)(2,1)} %stack.2), calls=%async_computation | async-start | bytes 8388608 | tf_op jit(solution)/shard_map/all_to_all | solution.py:98
  91.5 1.8 gather_fusion
  93.3 2.0 select_select_fusion
  95.3 4.6 copy.52
  99.9 3.7 copy.60
  103.6 3.6 copy.62
  107.2 12.2 %fusion.17 = f32[512,16,16]{2,1,0:T(8,128)} fusion(f32[16,16,512]{1,0,2:T(8,128)} %copy.51, f32[16,16,512]{1,0,2:T(8,128)} %copy.52), kind=kOutput, calls=%fused_computation.66 | convolution fusion | flops 25165824 | bytes 1572864 | tf_op jit(solution)/shard_map/tsc,bsc->btc/dot_general | solution.py:91
  119.4 148.7 %all-gather.12.cloned.1.call-done = f32[1024,512]{1,0:T(8,128)} async-done(((f32[16,512]{1,0:T(8,128)}), f32[1024,512]{1,0:T(8,128)}) %all-gather.12.cloned.1.call-update) | async-done | bytes 2097168 | tf_op jit(solution)/shard_map/all_gather | solution.py:9
  268.1 130.9 %all-gather.14.cloned.1.call-done = f32[1024,512]{1,0:T(8,128)} async-done(((f32[16,512]{1,0:T(8,128)}), f32[1024,512]{1,0:T(8,128)}) %all-gather.14.cloned.1.call-update) | async-done | bytes 2097168 | tf_op jit(solution)/shard_map/all_gather | solution.py:9
  399.0 139.9 %all-gather.16.cloned.1.call-done = f32[1024,512]{1,0:T(8,128)} async-done(((f32[16,512]{1,0:T(8,128)}), f32[1024,512]{1,0:T(8,128)}) %all-gather.16.cloned.1.call-update) | async-done | bytes 2097168 | tf_op jit(solution)/shard_map/all_gather | solution.py:9
  538.9 139.8 %all-gather.18.cloned.1.call-done = f32[1024,512]{1,0:T(8,128)} async-done(((f32[16,512]{1,0:T(8,128)}), f32[1024,512]{1,0:T(8,128)}) %all-gather.18.cloned.1.call-update) | async-done | bytes 2097168 | tf_op jit(solution)/shard_map/all_gather | solution.py:9
  678.7 54.3 %while.42 = (s32[]{:T(128)}, f32[16,512]{1,0:T(8,128)S(1)}, f32[16,512]{1,0:T(8,128)S(1)}, s32[]{:T(128)}, f32[64,16,512]{2,1,0:T(8,128)}, /*index=5*/f32[64,16,...) while((s32[]{:T(128)}, f32[16,512]{1,0:T(8,128)S(1)}, ...), condition=%wide.region_4.5_spmd.clone, body=%wide.region_3.4_spmd.clone.sunk | while | flops 98308 | bytes 262277 | solution.py:18
  679.5 0.8 fusion.32
  680.4 0.8 fusion.32
  681.2 0.8 fusion.32
  685.5 0.9 fusion.32
  687.3 0.9 fusion.32
  696.8 0.9 fusion.32
  698.5 0.8 fusion.32
  705.4 0.8 fusion.32
  706.3 0.8 fusion.32
  707.1 0.8 fusion.32
  710.6 0.8 fusion.32
  712.3 0.8 fusion.32
  713.1 0.9 fusion.32
  716.6 0.8 fusion.32
  719.2 0.9 fusion.32
  726.1 0.8 fusion.32
  727.0 0.8 fusion.32
  733.3 3.7 copy.59
  737.0 3.7 copy.61
  740.7 9.5 %fusion.18 = f32[512,16,16]{2,1,0:T(8,128)S(1)} fusion(f32[16,16,512]{1,0,2:T(8,128)} %copy.59, f32[16,16,512]{1,0,2:T(8,128)} %copy.60), kind=kOutput, calls=%fused_computation.67 | convolution fusion | flops 25165824 | bytes 1572864 | tf_op jit(solution)/shard_map/tnc,bnc->btc/dot_general | solution.py:88
  750.2 8.6 %add_bitcast_fusion = f32[16,16,512]{1,0,2:T(8,128)} fusion(f32[512,16,16]{2,1,0:T(8,128)S(1)} %copy-done, f32[512,16,16]{2,1,0:T(8,128)S(1)} %fusion.18, f32[16,16,512]{1,0,2:T(8,128)S(1)} %copy-done.2, f32[16,16,512]{1,0,2:T(8,128)S(1)} %copy-done.1), kind=kOutput, calls=%fused_computation.19 | convolution fusion | flops 25427968 | bytes 2621440 | tf_op jit(solution)/shard_map/tnc,bnc->btc/dot_general | solution.py:88
  758.7 2.9 copy.63
  761.7 0.8 fusion.15
  762.5 38.3 %all-gather.10.cloned.1.call-done = bf16[256,4096]{1,0:T(8,128)(2,1)} async-done(((bf16[256,512]{1,0:T(8,128)(2,1)}), bf16[256,4096]{1,0:T(8,128)(2,1)}) %all-gather.10.cloned.1.call-update) | async-done | bytes 2097168 | tf_op jit(solution)/shard_map/all_gather | solution.py:96
  800.8 4.8 convolution_convert_fusion
  (153 shorter events, 55.5 us)
Async XLA Ops:
  6.5 4.9 copy-start.12
  6.5 4.9 copy-start.13
  6.5 4.9 copy-start.11
  6.5 261.6 %all-gather.12.cloned.1.call-start = ((), (), s32[]{:S(2)}) async-start(), calls=%async_computation.2 | async-start | bytes 2129920 | tf_op jit(solution)/shard_map/all_gather | solution.py:9
  48.8 20.5 %copy-start.10 = (bf16[64,512]{1,0:T(8,128)(2,1)S(1)}, bf16[64,512]{1,0:T(8,128)(2,1)}, u32[]{:S(2)}) copy-start(bf16[64,512]{1,0:T(8,128)(2,1)} %param.19) | copy-start | bytes 196612
  66.5 0.6 copy-start.5
  66.6 0.7 copy-start.6
  66.6 1.4 copy-start.3
  66.6 2.1 copy-start.4
  67.2 331.8 %all-gather.14.cloned.1.call-start = ((), (), s32[]{:S(2)}) async-start(), calls=%async_computation.3 | async-start | bytes 2129920 | tf_op jit(solution)/shard_map/all_gather | solution.py:9
  67.9 471.0 %all-gather.16.cloned.1.call-start = ((), (), s32[]{:S(2)}) async-start(), calls=%async_computation.4 | async-start | bytes 2129920 | tf_op jit(solution)/shard_map/all_gather | solution.py:9
  68.7 610.0 %all-gather.18.cloned.1.call-start = ((), (), s32[]{:S(2)}) async-start(), calls=%async_computation.5 | async-start | bytes 2129920 | tf_op jit(solution)/shard_map/all_gather | solution.py:9
  71.8 729.0 %all-to-all-start = ((bf16[64,64,512]{2,1,0:T(8,128)(2,1)}), bf16[64,64,512]{2,1,0:T(8,128)(2,1)}, u32[]{:S(2)}, u32[]{:S(2)}) async-start(bf16[64,64,512]{2,1,0:T(8,128)(2,1)} %stack.2), calls=%async_computation | async-start | bytes 8388608 | tf_op jit(solution)/shard_map/all_to_all | solution.py:98
  91.3 709.5 %all-gather.10.cloned.1.call-start = ((), (), s32[]{:S(2)}) async-start(), calls=%async_computation.1 | async-start | bytes 2359296 | tf_op jit(solution)/shard_map/all_gather | solution.py:96
  740.7 9.5 %copy-start = (f32[512,16,16]{2,1,0:T(8,128)S(1)}, f32[512,16,16]{2,1,0:T(8,128)}, u32[]{:S(2)}) copy-start(f32[512,16,16]{2,1,0:T(8,128)} %fusion.17) | copy-start | bytes 1572868
  740.7 9.5 %copy-start.1 = (f32[16,16,512]{1,0,2:T(8,128)S(1)}, f32[16,16,512]{1,0,2:T(8,128)}, u32[]{:S(2)}) copy-start(f32[16,16,512]{1,0,2:T(8,128)} %copy.62) | copy-start | bytes 1572868
  740.7 9.5 %copy-start.2 = (f32[16,16,512]{1,0,2:T(8,128)S(1)}, f32[16,16,512]{1,0,2:T(8,128)}, u32[]{:S(2)}) copy-start(f32[16,16,512]{1,0,2:T(8,128)} %copy.61) | copy-start | bytes 1572868
  758.7 2.9 copy-start.7
  758.7 2.9 copy-start.8
  758.7 2.9 copy-start.9
  758.7 2.9 copy-start.14
Sparse Core Ops, SparseCore 0:
  67.3 200.7 all-gather.11
  271.1 127.8 all-gather.13
  401.9 136.9 all-gather.15
  541.7 136.9 all-gather.17
  762.6 38.1 all-gather.9
